TPU v7x, 256 devices: a whole 4x4x8 slice. The times are simulated.
256 devices in a mesh: win: 32 (over z, y_lo, core), chan: 8 (over x, y_hi).
Axes of the slice: x: 4, y: 4 (y_hi: 2, y_lo: 2; y = y_hi * 2 + y_lo), z: 8, core: 2. Of those that a mesh axis runs over, the one named last changes fastest.
Arguments:
- traces: bfloat16 [256, 1024, 4096], P('win', 'chan'), may hold values from -6 to 6
- source_block: int32 [3], replicated, may hold values from 0 to 7, as said below
- pair_source: int32 [3, 4096], P(None, 'chan'), may hold values from 0 to 127
- pair_receiver: int32 [3, 4096], P(None, 'chan'), may hold values from 0 to 127
- pair_bin: int32 [3, 4096], P(None, 'chan'), may hold values from 0 to 1023, as said below
- bin_slot: int32 [1024], replicated, may hold values from 0 to 1023, as said below
Outputs:
- stacks: float32 [3, 4096, 1024], P(None, 'win', 'chan')
Inputs may be any that keep to these rules, and one draw needn't show every extreme that they name: `source_block`: not every step names the same block; some step names block 0 and some step block 8 - 1. `pair_bin`: among the 512 pairs of one index of chan in a step, at most 128 have bins with bin_slot // 128 equal to one owner; in every step one owner gets exactly 128 from every index of chan. `bin_slot`: each bin has its own row.
All inputs are finite; a program needn't handle non-finite values.
Results may differ from a plain program's by a relative error of at most 0.0056.
Values may be sent and summed in bfloat16 or wider, within the bound.
No kernel may reach another device: no remote copies, remote signals or barrier semaphores. Data moves between devices by JAX's collectives and lax.ppermute only.
A program may use at most 64 MiB of HBM per device.

v0:
```python
import math
import jax
import jax.numpy as jnp
from jax import lax
from jax.sharding import PartitionSpec as P

WLEN = 4096
F = 128
FREQ0 = 256
LAGS = 4096
BIN_DEV = 128
STEPS = 3
P_DEV = 512


def from_root(block, axis, holder):
    block = jnp.where(lax.axis_index(axis) == holder, block, jnp.zeros_like(block))
    return lax.psum(block, axis)


def forward_table():
    samples = jnp.arange(WLEN, dtype=jnp.int32)
    freq_ids = FREQ0 + jnp.arange(F, dtype=jnp.int32)
    phases = samples[:, None] * freq_ids[None, :] % WLEN
    angles = phases.astype(jnp.float32) * (2.0 * math.pi / WLEN)
    return jnp.concatenate([jnp.cos(angles), -jnp.sin(angles)], axis=1).astype(jnp.bfloat16)


def lag_table(length, norm_scale):
    samples = jnp.arange(length, dtype=jnp.int32)
    freq_ids = FREQ0 + jnp.arange(F, dtype=jnp.int32)
    phases = freq_ids[:, None] * (samples[None, :] + (WLEN - LAGS // 2)) % WLEN
    angles = phases.astype(jnp.float32) * (2.0 * math.pi / WLEN)
    return jnp.concatenate([jnp.cos(angles), -jnp.sin(angles)], axis=0) * norm_scale


def cross_spectra(src_spec, rec_spec):
    src_re, src_im = (src_spec[..., :F], src_spec[..., F:])
    rec_re, rec_im = (rec_spec[..., :F], rec_spec[..., F:])
    real_part = jnp.sum(src_re * rec_re + src_im * rec_im, axis=0)
    imag_part = jnp.sum(src_re * rec_im - src_im * rec_re, axis=0)
    return jnp.concatenate([real_part, imag_part], axis=-1)


def project_lags(lag_basis, binned):
    return lax.dot_general(
        lag_basis, binned, (((0,), (1,)), ((), ())), precision=lax.Precision.HIGHEST
    )


def pick_channels(block, picks):
    chooser = (picks[:, None] == jnp.arange(block.shape[1], dtype=jnp.int32)[None, :]).astype(
        jnp.bfloat16
    )
    return jnp.einsum("pc,wcf->wpf", chooser, block, preferred_element_type=jnp.float32)


def on_device(traces, source_block, pair_source, pair_receiver, pair_bin, bin_slot):
    win_local, chan_local, samples_count = traces.shape
    chan_count = lax.axis_size("chan")
    win_count = lax.axis_size("win")
    lag_count = LAGS // win_count
    norm_scale = 1.0 / math.sqrt(2.0 * F * win_count * win_local)
    capacity = min(2 * P_DEV // chan_count, 3 * P_DEV // 4)
    spectra = jnp.dot(
        traces.reshape(win_local * chan_local, samples_count),
        forward_table(),
        preferred_element_type=jnp.float32,
    )
    power = jnp.mean(spectra * spectra, axis=-1, keepdims=True)
    whitened = (
        (spectra * lax.rsqrt(power + 1e-06))
        .astype(jnp.bfloat16)
        .reshape(win_local, chan_local, 2 * F)
    )
    bin_range = jnp.arange(bin_slot.shape[0], dtype=jnp.int32)
    pair_range = jnp.arange(P_DEV, dtype=jnp.int32)
    lower_tri = (pair_range[None, :] <= pair_range[:, None]).astype(jnp.bfloat16)
    results = []
    for section_index in range(STEPS):
        source = from_root(whitened, "chan", source_block[section_index])
        src_spec = pick_channels(source, pair_source[section_index])
        rec_spec = pick_channels(whitened, pair_receiver[section_index])
        partial_value = cross_spectra(src_spec, rec_spec).astype(jnp.bfloat16)
        matches_bin = pair_bin[section_index][:, None] == bin_range[None, :]
        slot_ids = jnp.sum(jnp.where(matches_bin, bin_slot[None, :], 0), axis=1)
        owners = slot_ids // BIN_DEV
        row_in_owner = slot_ids % BIN_DEV
        matches = owners[:, None] == jnp.arange(chan_count, dtype=jnp.int32)[None, :]
        running = jnp.dot(
            lower_tri, matches.astype(jnp.bfloat16), preferred_element_type=jnp.float32
        ).astype(jnp.int32)
        position = jnp.sum(jnp.where(matches, running - 1, 0), axis=1)
        target = owners * capacity + position
        slot_range = jnp.arange(chan_count * capacity, dtype=jnp.int32)
        placed = slot_range[:, None] == target[None, :]
        outgoing = jnp.dot(
            placed.astype(jnp.bfloat16), partial_value, preferred_element_type=jnp.float32
        )
        outgoing = outgoing.astype(jnp.bfloat16).reshape(chan_count, capacity, 2 * F)
        labels = jnp.sum(jnp.where(placed, row_in_owner[None, :] + 1, 0), axis=1) - 1
        labels = labels.reshape(chan_count, capacity)
        incoming, received_rows = (
            lax.all_to_all(outgoing, "chan", split_axis=0, concat_axis=0, tiled=True),
            lax.all_to_all(labels, "chan", split_axis=0, concat_axis=0, tiled=True),
        )
        onehot = (
            received_rows.reshape(-1)[None, :] == jnp.arange(BIN_DEV, dtype=jnp.int32)[:, None]
        ).astype(jnp.bfloat16)
        binned = jnp.dot(onehot, incoming.reshape(-1, 2 * F), preferred_element_type=jnp.float32)
        stacked = lax.psum_scatter(
            project_lags(lag_table(lag_count * lax.axis_size("win"), norm_scale), binned),
            "win",
            scatter_dimension=0,
            tiled=True,
        )
        results.append(stacked)
    return jnp.stack(results)


def solution(mesh):
    placed = (P("win", "chan", None), P(), P(None, "chan"), P(None, "chan"), P(None, "chan"), P())
    return jax.shard_map(
        on_device, mesh=mesh, in_specs=placed, out_specs=P(None, "win", "chan"), check_vma=False
    )
```

profile of v0, /device:TPU:2, one launch (start us, length us, event | category | flops | bytes accessed | tf_op | source)
XLA Modules:
  0.0 528.6 jit_solution(2868573302361774314)
XLA Ops:
  6.5 8.6 %cosine_convert_fusion = (bf16[4096,128]{1,0:T(8,128)(2,1)S(1)}, bf16[4096,128]{1,0:T(8,128)(2,1)S(1)}) fusion(s32[128]{0:T(128)S(1)} %iota_add_fusion.1), kind=kLoop, calls=%fused_computation.45 | loop fusion | flops 8912896 | bytes 2097664 | tf_op jit(solution)/shard_map/convert.6
  15.1 0.0 copy-start.6
  15.1 5.8 %multiply_reduce_fusion = (f32[1024]{0:T(1024)S(1)}, f32[256,1024]{1,0:T(8,128)S(1)}) fusion(bf16[1024,4096]{1,0:T(8,128)(2,1)} %bitcast.102, bf16[4096,128]{1,0:T(8,128)(2,1)S(1)} %get-tuple-element.41, bf16[4096,128]{1,0:T(8,128)(2,1)S(1)} %get-tuple-element.40), kind=kOutput, calls=%fused_computation.76 | convolution fusion | flops 2152201216 | bytes 11538432 | tf_op jit(solution)/shard_map/dot_general | solution.py:65
  21.0 0.7 fusion.100
  23.5 0.0 copy-start.3
  23.5 0.0 copy-start.7
  23.5 0.0 copy-start.4
  23.6 0.0 copy-start.5
  23.6 1.4 bitcast_select_fusion.2
  25.0 0.0 all-reduce.3.cloned.1.call-update
  25.0 1.2 select_reduce_fusion.5
  26.2 0.3 fusion.31
  26.5 0.3 select_reduce_fusion.4
  26.8 0.6 broadcast_add_fusion.2
  27.4 7.5 %all-to-all-start = ((s32[8,1,128]{2,1,0:T(1,128)}), s32[8,1,128]{2,1,0:T(1,128)S(1)}, u32[]{:S(2)}, u32[]{:S(2)}) async-start(s32[8,1,128]{2,1,0:T(1,128)} %bitcast.1), calls=%async_computation | async-start | bytes 8192 | tf_op jit(solution)/shard_map/all_to_all | solution.py:105
  34.9 0.1 fusion.38
  35.1 2.7 convolution_bitcast_fusion.4
  37.8 92.9 %all-reduce.3.cloned.1.call-done = (bf16[8,128,256]{1,2,0:T(8,128)(2,1)}, bf16[8,128,256]{1,2,0:T(8,128)(2,1)}, bf16[8,128,256]{1,2,0:T(8,128)(2,1)}) async-done(((bf16[8,128,256]{1,2,0:T(8,128)(2,1)}, bf16[8,128,256]{1,2,0:T(8,128)(2,1)}, bf16[8,128,256]{1,2,0:T(8,128)(2,1)}), (bf16[8,128,256]{1,2,0:T(8,128)(2,1)}, bf16[8,128,256]{1,2,0:T(8,128)(2,1)}, ...) | async-done | bytes 1572880 | tf_op jit(solution)/shard_map/psum | solution.py:18
  130.7 2.0 convolution_bitcast_fusion.5
  132.7 0.3 copy-done
  133.1 1.1 add_reduce_fusion.2
  134.2 1.3 fusion.22
  135.5 0.0 all-to-all-done
  135.5 5.5 %all-to-all-start.1 = ((bf16[8,128,256]{2,1,0:T(8,128)(2,1)}), bf16[8,128,256]{2,1,0:T(8,128)(2,1)S(1)}, u32[]{:S(2)}, u32[]{:S(2)}) async-start(bf16[8,128,256]{2,1,0:T(8,128)(2,1)} %bitcast.12), calls=%async_computation.1 | async-start | bytes 1048576 | tf_op jit(solution)/shard_map/all_to_all | solution.py:104
  141.0 0.5 reduce-scatter.4.cloned.1.call-start
  141.5 9.4 %fusion.37 = (f32[128,4096]{1,0:T(8,128)S(1)}, f32[128,4096]{1,0:T(8,128)}) fusion(s32[4096]{0:T(1024)S(1)} %iota_add_fusion, s32[128]{0:T(128)S(1)} %iota_add_fusion.1), kind=kLoop, calls=%fused_computation.79 | loop fusion | flops 7864320 | bytes 4211200 | tf_op jit(solution)/shard_map/cos | solution.py:34
  150.9 0.0 all-to-all-done.1
  150.9 0.2 fusion.42
  151.1 9.6 %fusion.2 = f32[4096,128]{1,0:T(8,128)} fusion(f32[128,256]{1,0:T(8,128)S(1)} %fusion.42, f32[128,4096]{1,0:T(8,128)} %get-tuple-element.21, f32[128,4096]{1,0:T(8,128)S(1)} %get-tuple-element.20), kind=kOutput, calls=%fused_computation.11 | convolution fusion | flops 1612709888 | bytes 6422528 | tf_op jit(solution)/shard_map/dot_general | solution.py:46
  160.7 0.0 reduce-scatter.4.cloned.1.call-update
  160.7 0.3 fusion.32
  161.0 0.3 select_reduce_fusion.2
  161.3 0.6 broadcast_add_fusion.1
  161.9 7.2 %all-to-all-start.2 = ((s32[8,1,128]{2,1,0:T(1,128)}), s32[8,1,128]{2,1,0:T(1,128)S(1)}, u32[]{:S(2)}, u32[]{:S(2)}) async-start(s32[8,1,128]{2,1,0:T(1,128)} %bitcast.16), calls=%async_computation.3 | async-start | bytes 8192 | tf_op jit(solution)/shard_map/all_to_all | solution.py:105
  169.1 0.2 reduce-scatter.6.cloned.1.call-start
  169.3 0.8 convolution_bitcast_fusion.2
  170.1 0.2 copy-done.2
  170.3 0.8 convolution_bitcast_fusion.3
  171.2 1.1 add_reduce_fusion.1
  172.2 0.5 fusion.23
  172.8 2.5 all-to-all-done.2
  175.2 13.2 %all_to_all.33 = bf16[8,128,256]{2,1,0:T(8,128)(2,1)S(1)} all-to-all(bf16[8,128,256]{2,1,0:T(8,128)(2,1)S(1)} %bitcast.85), channel_id=1, replica_groups=mesh['win'=32,'chan'=8] {'chan'}, dimensions={0} | all-to-all | bytes 1048576 | tf_op jit(solution)/shard_map/all_to_all | solution.py:104
  188.5 0.2 fusion.43
  188.7 9.6 %fusion.1 = f32[4096,128]{1,0:T(8,128)} fusion(f32[128,256]{1,0:T(8,128)S(1)} %fusion.43, f32[128,4096]{1,0:T(8,128)} %get-tuple-element.21, f32[128,4096]{1,0:T(8,128)S(1)} %get-tuple-element.20), kind=kOutput, calls=%fused_computation.10 | convolution fusion | flops 1612709888 | bytes 6422528 | tf_op jit(solution)/shard_map/dot_general | solution.py:46
  198.3 0.0 reduce-scatter.6.cloned.1.call-update
  198.4 0.3 fusion.33
  198.7 0.3 select_reduce_fusion
  199.0 0.6 broadcast_add_fusion
  199.6 4.8 all-to-all-start.4
  204.3 0.2 reduce-scatter.8.cloned.1.call-start
  204.6 0.8 convolution_bitcast_fusion
  205.4 0.2 copy-done.1
  205.6 0.8 convolution_bitcast_fusion.1
  206.4 1.1 add_reduce_fusion
  207.5 0.5 fusion.24
  208.0 2.4 all-to-all-done.4
  210.5 12.6 %all_to_all.34 = bf16[8,128,256]{2,1,0:T(8,128)(2,1)S(1)} all-to-all(bf16[8,128,256]{2,1,0:T(8,128)(2,1)S(1)} %bitcast.86), channel_id=1, replica_groups=mesh['win'=32,'chan'=8] {'chan'}, dimensions={0} | all-to-all | bytes 1048576 | tf_op jit(solution)/shard_map/all_to_all | solution.py:104
  223.1 0.2 fusion.44
  223.3 9.6 %fusion = f32[4096,128]{1,0:T(8,128)} fusion(f32[128,256]{1,0:T(8,128)S(1)} %fusion.44, f32[128,4096]{1,0:T(8,128)} %get-tuple-element.21, f32[128,4096]{1,0:T(8,128)S(1)} %get-tuple-element.20), kind=kOutput, calls=%fused_computation.9 | convolution fusion | flops 1612709888 | bytes 6422528 | tf_op jit(solution)/shard_map/dot_general | solution.py:46
  233.0 0.0 reduce-scatter.8.cloned.1.call-update
  233.0 48.9 %reduce-scatter.4.cloned.1.call-done = f32[128,128]{1,0:T(8,128)} async-done(((f32[4096,128]{1,0:T(8,128)}), f32[128,128]{1,0:T(8,128)}) %reduce-scatter.4.cloned.1.call-update) | async-done | bytes 65552 | tf_op jit(solution)/shard_map/reduce_scatter | solution.py:111
  281.9 119.5 %reduce-scatter.6.cloned.1.call-done = f32[128,128]{1,0:T(8,128)} async-done(((f32[4096,128]{1,0:T(8,128)}), f32[128,128]{1,0:T(8,128)}) %reduce-scatter.6.cloned.1.call-update) | async-done | bytes 65552 | tf_op jit(solution)/shard_map/reduce_scatter | solution.py:111
  401.4 118.8 %reduce-scatter.8.cloned.1.call-done = f32[128,128]{1,0:T(8,128)} async-done(((f32[4096,128]{1,0:T(8,128)}), f32[128,128]{1,0:T(8,128)}) %reduce-scatter.8.cloned.1.call-update) | async-done | bytes 65552 | tf_op jit(solution)/shard_map/reduce_scatter | solution.py:111
  520.2 1.6 pad_maximum_fusion
  (20 shorter events, 0.1 us)
Async XLA Ops:
  6.5 124.2 %all-reduce.3.cloned.1.call-start = ((), (), s32[]{:S(2)}) async-start(), calls=%async_computation.12 | async-start | bytes 3145728 | tf_op jit(solution)/shard_map/psum | solution.py:18
  15.1 5.8 %copy-start.6 = (s32[3]{0:T(128)S(1)}, s32[3]{0:T(128)}, u32[]{:S(2)}) copy-start(s32[3]{0:T(128)} %param.7) | copy-start | bytes 40
  23.5 1.5 copy-start.3
  23.5 1.5 copy-start.7
  23.5 11.3 %copy-start.4 = (s32[3,512]{1,0:T(4,128)S(1)}, s32[3,512]{1,0:T(4,128)}, u32[]{:S(2)}) copy-start(s32[3,512]{1,0:T(4,128)} %param.8) | copy-start | bytes 18436
  23.6 11.3 %copy-start.5 = (s32[3,512]{1,0:T(4,128)S(1)}, s32[3,512]{1,0:T(4,128)}, u32[]{:S(2)}) copy-start(s32[3,512]{1,0:T(4,128)} %param.9) | copy-start | bytes 18436
  27.4 108.1 %all-to-all-start = ((s32[8,1,128]{2,1,0:T(1,128)}), s32[8,1,128]{2,1,0:T(1,128)S(1)}, u32[]{:S(2)}, u32[]{:S(2)}) async-start(s32[8,1,128]{2,1,0:T(1,128)} %bitcast.1), calls=%async_computation | async-start | bytes 8192 | tf_op jit(solution)/shard_map/all_to_all | solution.py:105
  130.7 2.3 copy-start
  135.5 15.4 %all-to-all-start.1 = ((bf16[8,128,256]{2,1,0:T(8,128)(2,1)}), bf16[8,128,256]{2,1,0:T(8,128)(2,1)S(1)}, u32[]{:S(2)}, u32[]{:S(2)}) async-start(bf16[8,128,256]{2,1,0:T(8,128)(2,1)} %bitcast.12), calls=%async_computation.1 | async-start | bytes 1048576 | tf_op jit(solution)/shard_map/all_to_all | solution.py:104
  141.0 140.8 %reduce-scatter.4.cloned.1.call-start = ((), (), s32[]{:S(2)}) async-start(), calls=%async_computation.9 | async-start | bytes 2162688 | tf_op jit(solution)/shard_map/reduce_scatter | solution.py:111
  161.9 13.3 %all-to-all-start.2 = ((s32[8,1,128]{2,1,0:T(1,128)}), s32[8,1,128]{2,1,0:T(1,128)S(1)}, u32[]{:S(2)}, u32[]{:S(2)}) async-start(s32[8,1,128]{2,1,0:T(1,128)} %bitcast.16), calls=%async_computation.3 | async-start | bytes 8192 | tf_op jit(solution)/shard_map/all_to_all | solution.py:105
  169.1 232.2 %reduce-scatter.6.cloned.1.call-start = ((), (), s32[]{:S(2)}) async-start(), calls=%async_computation.10 | async-start | bytes 2162688 | tf_op jit(solution)/shard_map/reduce_scatter | solution.py:111
  169.3 1.0 copy-start.2
  199.6 10.9 %all-to-all-start.4 = ((s32[8,1,128]{2,1,0:T(1,128)}), s32[8,1,128]{2,1,0:T(1,128)S(1)}, u32[]{:S(2)}, u32[]{:S(2)}) async-start(s32[8,1,128]{2,1,0:T(1,128)} %bitcast.29), calls=%async_computation.6 | async-start | bytes 8192 | tf_op jit(solution)/shard_map/all_to_all | solution.py:105
  204.3 315.9 %reduce-scatter.8.cloned.1.call-start = ((), (), s32[]{:S(2)}) async-start(), calls=%async_computation.11 | async-start | bytes 2162688 | tf_op jit(solution)/shard_map/reduce_scatter | solution.py:111
  204.6 1.0 copy-start.1
Sparse Core Ops, SparseCore 0:
  25.1 105.5 all-reduce.2
  160.9 120.9 reduce-scatter.3
  284.6 116.7 reduce-scatter.5
  403.7 116.4 reduce-scatter.7
where the time goes:
time: 536 us; the launch traced here: 529 us
  waiting for transfers between devices  385 us (72%)
  matrix products  46.4 us (9%)
  other arithmetic  28.2 us (5%)
  starting transfers between devices  25.9 us (5%)
  blocking collectives  25.9 us (5%)
  between operations  15.5 us (3%)
    reduce_scatter x3, waiting for transfers between devices, on_device(): lax.psum_scatter(project_lags(lag_table(lag_count * lax.axis_size('win'),...  287 us
    psum x1, waiting for transfers between devices, from_root(): return lax.psum(block, axis)  92.9 us
    dot_general x3, matrix products, project_lags(): lax.dot_general(lag_basis, binned, (((0,), (1,)), ((), ())), precision=la...  28.8 us
    all_to_all x2, blocking collectives, on_device(): lax.all_to_all(outgoing, 'chan', split_axis=0, concat_axis=0, tiled=True)  25.9 us
    all_to_all x3, starting transfers between devices, on_device(): lax.all_to_all(labels, 'chan', split_axis=0, concat_axis=0, tiled=True)  19.5 us
  transfers between devices with their start and end apart: 8, of which 6 were waited for; matrix products, arithmetic and copies ran while one was open for 9% of the time, Pallas kernels for 0%

commit v1 on v0

--- a/solution.py
+++ b/solution.py
@@ -15,7 +15,7 @@
 
 def from_root(block, axis, holder):
     block = jnp.where(lax.axis_index(axis) == holder, block, jnp.zeros_like(block))
-    return lax.psum(block, axis)
+    return jnp.sum(lax.all_gather(block, axis_name=axis), axis=0)
 
 
 def forward_table():

time: 536 us -> 635 us (1.18)
  waiting for transfers between devices: 385 us -> 464 us
  other arithmetic: 28.2 us -> 35.9 us
    all_gather x0 -> x3, waiting for transfers between devices: none -> 134 us  [from_root(): return jnp.sum(lax.all_gather(block, axis_name=axis), axis=0)]
    psum x1 -> x0, waiting for transfers between devices: 92.9 us -> none  [from_root(): return lax.psum(block, axis)]
    reduce_scatter x3, waiting for transfers between devices: 287 us -> 328 us  [on_device(): lax.psum_scatter(project_lags(lag_table(lag_count * lax.axis_size('win'),...]
    reduce_sum x0 -> x3, other arithmetic: none -> 8.9 us  [from_root(): return jnp.sum(lax.all_gather(block, axis_name=axis), axis=0)]
  transfers between devices with their start and end apart: 8 -> 10, of which waited for: 6 -> 7; matrix products, arithmetic and copies ran while one was open for 9% -> 11% of each run, Pallas kernels for 0% -> 0%
where the time goes in v1:
time: 635 us; the launch traced here: 627 us
  waiting for transfers between devices  464 us (73%)
  matrix products  49.3 us (8%)
  other arithmetic  35.9 us (6%)
  blocking collectives  28.3 us (4%)
  starting transfers between devices  26.2 us (4%)
  between operations  16 us (3%)
  local copies, waits for them, and re-layouts  7.75 us (1%)
    reduce_scatter x3, waiting for transfers between devices, on_device(): lax.psum_scatter(project_lags(lag_table(lag_count * lax.axis_size('win'),...  328 us
    all_gather x3, waiting for transfers between devices, from_root(): return jnp.sum(lax.all_gather(block, axis_name=axis), axis=0)  134 us
    dot_general x3, matrix products, project_lags(): lax.dot_general(lag_basis, binned, (((0,), (1,)), ((), ())), precision=la...  28.9 us
    all_to_all x2, blocking collectives, on_device(): lax.all_to_all(outgoing, 'chan', split_axis=0, concat_axis=0, tiled=True)  28.3 us
    all_to_all x3, starting transfers between devices, on_device(): lax.all_to_all(labels, 'chan', split_axis=0, concat_axis=0, tiled=True)  20.1 us
  transfers between devices with their start and end apart: 10, of which 7 were waited for; matrix products, arithmetic and copies ran while one was open for 11% of the time, Pallas kernels for 0%

profile of v1, /device:TPU:2, one launch (start us, length us, event | category | flops | bytes accessed | tf_op | source)
XLA Modules:
  0.0 627.0 jit_solution(4389534270755572728)
XLA Ops:
  6.5 8.6 %cosine_convert_fusion = (bf16[4096,128]{1,0:T(8,128)(2,1)S(1)}, bf16[4096,128]{1,0:T(8,128)(2,1)S(1)}) fusion(s32[128]{0:T(128)S(1)} %iota_add_fusion.1), kind=kLoop, calls=%fused_computation.45 | loop fusion | flops 8912896 | bytes 2097664 | tf_op jit(solution)/shard_map/convert.9
  15.1 5.8 multiply_reduce_fusion
  21.0 0.6 fusion.99
  22.3 0.2 bitcast_select_fusion.2
  22.5 1.0 copy.34
  23.5 0.0 all-gather.4.cloned.1.call-update
  23.5 0.0 all-gather.6.cloned.1.call-start
  24.8 0.1 bitcast_select_fusion
  24.9 1.0 copy.35
  26.0 0.0 all-gather.6.cloned.1.call-update
  26.0 0.0 all-gather.8.cloned.1.call-start
  26.0 1.0 copy.36
  27.1 1.2 select_reduce_fusion.5
  28.3 0.3 fusion.31
  28.6 0.3 select_reduce_fusion.4
  28.9 0.6 broadcast_add_fusion.2
  29.5 7.5 %all-to-all-start = ((s32[8,1,128]{2,1,0:T(1,128)}), s32[8,1,128]{2,1,0:T(1,128)S(1)}, u32[]{:S(2)}, u32[]{:S(2)}) async-start(s32[8,1,128]{2,1,0:T(1,128)} %bitcast.1), calls=%async_computation | async-start | bytes 8192 | tf_op jit(solution)/shard_map/all_to_all | solution.py:105
  37.0 2.8 convolution_bitcast_fusion.4
  39.8 62.3 %all-gather.4.cloned.1.call-done = bf16[8,8,128,256]{3,2,1,0:T(8,128)(2,1)} async-done(((bf16[1,8,128,256]{3,2,1,0:T(8,128)(2,1)}), bf16[8,8,128,256]{3,2,1,0:T(8,128)(2,1)}) %all-gather.4.cloned.1.call-update) | async-done | bytes 4194320 | tf_op jit(solution)/shard_map/all_gather | solution.py:18
  102.1 3.0 reduce_sum.184
  105.1 0.8 convolution_bitcast_fusion.5
  105.9 1.3 copy-done.1
  107.3 1.1 add_reduce_fusion.2
  108.4 1.3 fusion.22
  109.7 5.2 all-to-all-start.1
  114.8 0.5 reduce-scatter.4.cloned.1.call-start
  115.3 9.4 %fusion.37 = (f32[128,4096]{1,0:T(8,128)S(1)}, f32[128,4096]{1,0:T(8,128)}) fusion(s32[4096]{0:T(1024)S(1)} %iota_add_fusion, s32[128]{0:T(128)S(1)} %iota_add_fusion.1), kind=kLoop, calls=%fused_computation.79 | loop fusion | flops 7864320 | bytes 4211200 | tf_op jit(solution)/shard_map/cos | solution.py:34
  124.7 1.6 all-to-all-done.1
  126.2 0.2 fusion.41
  126.5 9.6 %fusion.2 = f32[4096,128]{1,0:T(8,128)} fusion(f32[128,256]{1,0:T(8,128)S(1)} %fusion.41, f32[128,4096]{1,0:T(8,128)} %get-tuple-element.19, f32[128,4096]{1,0:T(8,128)S(1)} %get-tuple-element.18), kind=kOutput, calls=%fused_computation.11 | convolution fusion | flops 1612709888 | bytes 6422528 | tf_op jit(solution)/shard_map/dot_general | solution.py:46
  136.1 0.3 fusion.32
  136.4 0.3 select_reduce_fusion.2
  136.7 0.6 broadcast_add_fusion.1
  137.3 6.5 %all-to-all-start.2 = ((s32[8,1,128]{2,1,0:T(1,128)}), s32[8,1,128]{2,1,0:T(1,128)S(1)}, u32[]{:S(2)}, u32[]{:S(2)}) async-start(s32[8,1,128]{2,1,0:T(1,128)} %bitcast.17), calls=%async_computation.3 | async-start | bytes 8192 | tf_op jit(solution)/shard_map/all_to_all | solution.py:105
  143.8 0.2 reduce-scatter.6.cloned.1.call-start
  144.0 2.8 convolution_bitcast_fusion.2
  146.8 34.4 %all-gather.6.cloned.1.call-done = bf16[8,8,128,256]{3,2,1,0:T(8,128)(2,1)} async-done(((bf16[1,8,128,256]{3,2,1,0:T(8,128)(2,1)}), bf16[8,8,128,256]{3,2,1,0:T(8,128)(2,1)}) %all-gather.6.cloned.1.call-update) | async-done | bytes 4194320 | tf_op jit(solution)/shard_map/all_gather | solution.py:18
  181.2 3.0 reduce_sum.190
  184.2 0.8 convolution_bitcast_fusion.3
  185.0 1.3 copy-done.2
  186.4 1.1 add_reduce_fusion.1
  187.5 0.5 fusion.23
  188.0 14.0 %all_to_all.33 = bf16[8,128,256]{2,1,0:T(8,128)(2,1)S(1)} all-to-all(bf16[8,128,256]{2,1,0:T(8,128)(2,1)S(1)} %bitcast.98), channel_id=1, replica_groups=mesh['win'=32,'chan'=8] {'chan'}, dimensions={0} | all-to-all | bytes 1048576 | tf_op jit(solution)/shard_map/all_to_all | solution.py:104
  202.0 0.2 fusion.42
  202.2 9.7 %fusion.1 = f32[4096,128]{1,0:T(8,128)} fusion(f32[128,256]{1,0:T(8,128)S(1)} %fusion.42, f32[128,4096]{1,0:T(8,128)} %get-tuple-element.19, f32[128,4096]{1,0:T(8,128)S(1)} %get-tuple-element.18), kind=kOutput, calls=%fused_computation.10 | convolution fusion | flops 1612709888 | bytes 6422528 | tf_op jit(solution)/shard_map/dot_general | solution.py:46
  212.0 0.3 fusion.33
  212.2 0.3 select_reduce_fusion
  212.5 0.6 broadcast_add_fusion
  213.1 6.1 all-to-all-start.4
  219.3 0.2 reduce-scatter.8.cloned.1.call-start
  219.5 2.8 convolution_bitcast_fusion
  222.3 37.0 %all-gather.8.cloned.1.call-done = bf16[8,8,128,256]{3,2,1,0:T(8,128)(2,1)} async-done(((bf16[1,8,128,256]{3,2,1,0:T(8,128)(2,1)}), bf16[8,8,128,256]{3,2,1,0:T(8,128)(2,1)}) %all-gather.8.cloned.1.call-update) | async-done | bytes 4194320 | tf_op jit(solution)/shard_map/all_gather | solution.py:18
  259.3 3.0 reduce_sum.196
  262.2 0.8 convolution_bitcast_fusion.1
  263.1 1.3 copy-done
  264.4 1.1 add_reduce_fusion
  265.5 0.5 fusion.24
  266.0 14.4 %all_to_all.34 = bf16[8,128,256]{2,1,0:T(8,128)(2,1)S(1)} all-to-all(bf16[8,128,256]{2,1,0:T(8,128)(2,1)S(1)} %bitcast.99), channel_id=1, replica_groups=mesh['win'=32,'chan'=8] {'chan'}, dimensions={0} | all-to-all | bytes 1048576 | tf_op jit(solution)/shard_map/all_to_all | solution.py:104
  280.4 0.2 fusion.43
  280.6 9.6 %fusion = f32[4096,128]{1,0:T(8,128)} fusion(f32[128,256]{1,0:T(8,128)S(1)} %fusion.43, f32[128,4096]{1,0:T(8,128)} %get-tuple-element.19, f32[128,4096]{1,0:T(8,128)S(1)} %get-tuple-element.18), kind=kOutput, calls=%fused_computation.9 | convolution fusion | flops 1612709888 | bytes 6422528 | tf_op jit(solution)/shard_map/dot_general | solution.py:46
  290.2 89.3 %reduce-scatter.4.cloned.1.call-done = f32[128,128]{1,0:T(8,128)} async-done(((f32[4096,128]{1,0:T(8,128)}), f32[128,128]{1,0:T(8,128)}) %reduce-scatter.4.cloned.1.call-update) | async-done | bytes 65552 | tf_op jit(solution)/shard_map/reduce_scatter | solution.py:111
  379.6 119.5 %reduce-scatter.6.cloned.1.call-done = f32[128,128]{1,0:T(8,128)} async-done(((f32[4096,128]{1,0:T(8,128)}), f32[128,128]{1,0:T(8,128)}) %reduce-scatter.6.cloned.1.call-update) | async-done | bytes 65552 | tf_op jit(solution)/shard_map/reduce_scatter | solution.py:111
  499.1 119.3 %reduce-scatter.8.cloned.1.call-done = f32[128,128]{1,0:T(8,128)} async-done(((f32[4096,128]{1,0:T(8,128)}), f32[128,128]{1,0:T(8,128)}) %reduce-scatter.8.cloned.1.call-update) | async-done | bytes 65552 | tf_op jit(solution)/shard_map/reduce_scatter | solution.py:111
  618.3 1.6 pad_maximum_fusion
  (32 shorter events, 0.2 us)
Async XLA Ops:
  6.5 95.6 %all-gather.4.cloned.1.call-start = ((), (), s32[]{:S(2)}) async-start(), calls=%async_computation.9 | async-start | bytes 4718592 | tf_op jit(solution)/shard_map/all_gather | solution.py:18
  15.1 5.8 copy-start.6
  23.5 157.7 %all-gather.6.cloned.1.call-start = ((), (), s32[]{:S(2)}) async-start(), calls=%async_computation.11 | async-start | bytes 4718592 | tf_op jit(solution)/shard_map/all_gather | solution.py:18
  24.8 2.2 copy-start.3
  24.8 2.3 copy-start.7
  24.9 12.0 %copy-start.4 = (s32[3,512]{1,0:T(4,128)S(1)}, s32[3,512]{1,0:T(4,128)}, u32[]{:S(2)}) copy-start(s32[3,512]{1,0:T(4,128)} %param.9) | copy-start | bytes 18436
  24.9 12.0 %copy-start.5 = (s32[3,512]{1,0:T(4,128)S(1)}, s32[3,512]{1,0:T(4,128)}, u32[]{:S(2)}) copy-start(s32[3,512]{1,0:T(4,128)} %param.8) | copy-start | bytes 18436
  26.0 233.3 %all-gather.8.cloned.1.call-start = ((), (), s32[]{:S(2)}) async-start(), calls=%async_computation.13 | async-start | bytes 4718592 | tf_op jit(solution)/shard_map/all_gather | solution.py:18
  29.5 80.2 %all-to-all-start = ((s32[8,1,128]{2,1,0:T(1,128)}), s32[8,1,128]{2,1,0:T(1,128)S(1)}, u32[]{:S(2)}, u32[]{:S(2)}) async-start(s32[8,1,128]{2,1,0:T(1,128)} %bitcast.1), calls=%async_computation | async-start | bytes 8192 | tf_op jit(solution)/shard_map/all_to_all | solution.py:105
  105.1 2.2 copy-start.1
  109.7 16.6 %all-to-all-start.1 = ((bf16[8,128,256]{2,1,0:T(8,128)(2,1)}), bf16[8,128,256]{2,1,0:T(8,128)(2,1)S(1)}, u32[]{:S(2)}, u32[]{:S(2)}) async-start(bf16[8,128,256]{2,1,0:T(8,128)(2,1)} %bitcast.13), calls=%async_computation.1 | async-start | bytes 1048576 | tf_op jit(solution)/shard_map/all_to_all | solution.py:104
  114.8 264.7 %reduce-scatter.4.cloned.1.call-start = ((), (), s32[]{:S(2)}) async-start(), calls=%async_computation.10 | async-start | bytes 2162688 | tf_op jit(solution)/shard_map/reduce_scatter | solution.py:111
  137.3 50.7 %all-to-all-start.2 = ((s32[8,1,128]{2,1,0:T(1,128)}), s32[8,1,128]{2,1,0:T(1,128)S(1)}, u32[]{:S(2)}, u32[]{:S(2)}) async-start(s32[8,1,128]{2,1,0:T(1,128)} %bitcast.17), calls=%async_computation.3 | async-start | bytes 8192 | tf_op jit(solution)/shard_map/all_to_all | solution.py:105
  143.8 355.3 %reduce-scatter.6.cloned.1.call-start = ((), (), s32[]{:S(2)}) async-start(), calls=%async_computation.12 | async-start | bytes 2162688 | tf_op jit(solution)/shard_map/reduce_scatter | solution.py:111
  184.2 2.2 copy-start.2
  213.1 52.9 %all-to-all-start.4 = ((s32[8,1,128]{2,1,0:T(1,128)}), s32[8,1,128]{2,1,0:T(1,128)S(1)}, u32[]{:S(2)}, u32[]{:S(2)}) async-start(s32[8,1,128]{2,1,0:T(1,128)} %bitcast.31), calls=%async_computation.6 | async-start | bytes 8192 | tf_op jit(solution)/shard_map/all_to_all | solution.py:105
  219.3 399.1 %reduce-scatter.8.cloned.1.call-start = ((), (), s32[]{:S(2)}) async-start(), calls=%async_computation.14 | async-start | bytes 2162688 | tf_op jit(solution)/shard_map/reduce_scatter | solution.py:111
  262.2 2.2 copy-start
Sparse Core Ops, SparseCore 0:
  23.6 78.4 all-gather.3
  104.7 76.4 all-gather.5
  183.9 75.3 all-gather.7
  261.6 117.8 reduce-scatter.3
  382.1 116.9 reduce-scatter.5
  501.5 116.8 reduce-scatter.7
